TPU v7x, 256 devices: a whole 4x4x8 slice. The times are simulated.
256 devices in a mesh: grp: 32 (over x_hi, z, core), rep: 8 (over x_lo, y).
Axes of the slice: x: 4 (x_hi: 2, x_lo: 2; x = x_hi * 2 + x_lo), y: 4, z: 8, core: 2. Of those that a mesh axis runs over, the one named last changes fastest.
Arguments:
- features: bfloat16 [24576, 512], P(('grp', 'rep')), may hold values from -6 to 6
- tile_values: bfloat16 [768, 32, 2, 128, 128], P(('grp', 'rep')), may hold values from 0.019897461 to 1
- tile_columns: int32 [768, 32, 2], P(('grp', 'rep')), may hold values from 0 to 5, as said below
- tile_counts: int32 [768, 32], P(('grp', 'rep')), may hold values from 0 to 2
- state_ids: int32 [98304], P(('grp', 'rep')), may hold values from 0 to 24575
- self_weight: bfloat16 [512, 512], replicated, may hold values from -0.25 to 0.25
- neighbour_weight: bfloat16 [512, 512], replicated, may hold values from -0.25 to 0.25
- bias_vector: float32 [512], replicated, may hold values from -3 to 3
Outputs:
- embedded: bfloat16 [98304, 512], P(('grp', 'rep'))
Inputs may be any that keep to these rules, and one draw needn't show every extreme that they name: `tile_columns`: for each row block and group the first tile_counts entries name distinct column blocks of that group; entries beyond the count are padding and are ignored.
All inputs are finite; a program needn't handle non-finite values.
Results may differ from a plain program's by a relative error of at most 0.0033.
Values may be sent and summed in bfloat16 or wider, within the bound.
A program may use at most 192 MiB of HBM per device.

v0:
```python
import jax
import jax.numpy as jnp
from jax import lax
from jax.sharding import PartitionSpec as P


def on_device(
    features,
    tile_values,
    tile_columns,
    tile_counts,
    state_ids,
    self_weight,
    neighbour_weight,
    bias_vector,
):
    panels = lax.all_gather(features, "rep", axis=0, tiled=True)
    row_blocks = tile_values.shape[0]
    group_count = tile_values.shape[1]
    slot_count = tile_values.shape[2]
    tile_size = tile_values.shape[3]
    panel_rows = panels.shape[0]
    width = panels.shape[1]
    panel_blocks = panel_rows // tile_size
    local_rows = row_blocks * tile_size
    positions = lax.broadcasted_iota(jnp.int32, (row_blocks, group_count, slot_count), 2)
    usable = positions < tile_counts[:, :, None]
    row_sums = jnp.sum(tile_values, axis=4, dtype=jnp.float32)
    degree = 1.0 + jnp.sum(
        jnp.where(usable[:, :, :, None], row_sums, jnp.float32(0.0)), axis=(1, 2)
    ).reshape(local_rows)
    masked_values = jnp.where(usable[:, :, :, None, None], tile_values, jnp.zeros((), jnp.bfloat16))
    block_iota = lax.broadcasted_iota(jnp.int32, (1, 1, panel_blocks), 2)
    zero_value = jnp.zeros((), jnp.bfloat16)

    def dense_group(group):
        columns = lax.dynamic_index_in_dim(tile_columns, group, 1, keepdims=False)
        values = lax.dynamic_index_in_dim(masked_values, group, 1, keepdims=False)
        hits = columns[:, :, None] == block_iota
        dense = jnp.zeros((row_blocks, tile_size, panel_blocks, tile_size), jnp.bfloat16)
        for slot in range(slot_count):
            placed = jnp.where(
                hits[:, slot, None, :, None], values[:, slot, :, None, :], zero_value
            )
            dense = dense + placed
        return dense.reshape(local_rows, panel_rows)

    def group_product(window, group, totals):
        dense = dense_group(group)
        return totals + jnp.dot(dense, window, preferred_element_type=jnp.float32)

    everything = lax.all_gather(panels, "grp", axis=0, tiled=True)

    def each_group(group, running):
        window = lax.dynamic_slice_in_dim(everything, group * panel_rows, panel_rows, 0)
        return group_product(window, group, running)

    totals = lax.fori_loop(0, group_count, each_group, jnp.zeros((local_rows, width), jnp.float32))
    own_rows = jnp.take(everything, state_ids, axis=0)
    neighbour = (totals / jnp.sqrt(degree)[:, None]).astype(jnp.bfloat16)
    activation = jnp.dot(own_rows, self_weight, preferred_element_type=jnp.float32)
    activation = activation + jnp.dot(
        neighbour, neighbour_weight, preferred_element_type=jnp.float32
    )
    activation = activation + bias_vector[None, :]
    return jnp.maximum(activation, 0.0).astype(jnp.bfloat16)


def solution(mesh):
    placed = (
        P(("grp", "rep"), None),
        P(("grp", "rep"), None, None, None, None),
        P(("grp", "rep"), None, None),
        P(("grp", "rep"), None),
        P(("grp", "rep")),
        P(),
        P(),
        P(),
    )
    return jax.shard_map(
        on_device, mesh=mesh, in_specs=placed, out_specs=P(("grp", "rep"), None), check_vma=False
    )
```

profile of v0, /device:TPU:1, one launch (start us, length us, event | category | flops | bytes accessed | tf_op | source)
XLA Modules:
  0.0 342.0 jit_solution(12657822559184209282)
XLA Ops:
  6.5 27.6 %all_gather.6 = bf16[768,512]{1,0:T(8,128)(2,1)} all-gather(bf16[96,512]{1,0:T(8,128)(2,1)} %param.10), channel_id=1, replica_groups=mesh['grp'=32,'rep'=8] {'rep'}, dimensions={0}, use_global_device_ids=true | all-gather | bytes 884736 | tf_op jit(solution)/shard_map/all_gather | solution.py:17
  36.9 4.7 %convert_reduce_fusion = f32[3,32,2,128]{3,2,1,0:T(2,128)S(1)} fusion(bf16[3,32,2,128,128]{4,3,2,1,0:T(8,128)(2,1)} %param.11), kind=kLoop, calls=%fused_computation.15 | loop fusion | flops 6266880 | bytes 6389760 | tf_op jit(solution)/shard_map/reduce_sum | solution.py:28
  41.9 3.1 copy_select_fusion
  44.9 178.6 %all-gather.2.cloned.1.call-done = bf16[24576,512]{1,0:T(8,128)(2,1)} async-done(((bf16[768,512]{1,0:T(8,128)(2,1)}), bf16[24576,512]{1,0:T(8,128)(2,1)}) %all-gather.2.cloned.1.call-update) | async-done | bytes 25165840 | tf_op jit(solution)/shard_map/all_gather | solution.py:52
  223.6 96.5 %while.14 = (s32[]{:T(128)}, f32[384,512]{1,0:T(8,128)S(1)}, s32[3,32,2]{0,2,1:T(2,128)S(1)}, bf16[3,32,2,128,128]{4,3,0,2,1:T(8,128)(2,1)}, bf16[24576,512]{1,0...) while((s32[]{:T(128)}, f32[384,512]{1,0:T(8,128)S(1)}, ...), condition=%wide.region_1.2_spmd.clone, body=%wide.region_0.0_spmd.clone.sunk | while | flops 303267872 | bytes 4522361 | solution.py:58
  223.6 1.0 dynamic-slice_bitcast_fusion.5
  224.9 1.7 convolution_add_fusion.3
  226.6 0.9 dynamic-slice_bitcast_fusion.5
  227.9 1.7 convolution_add_fusion.3
  229.6 0.9 dynamic-slice_bitcast_fusion.5
  231.0 1.7 convolution_add_fusion.3
  232.7 0.9 dynamic-slice_bitcast_fusion.5
  234.0 1.7 convolution_add_fusion.3
  235.7 0.9 dynamic-slice_bitcast_fusion.5
  237.0 1.7 convolution_add_fusion.3
  238.7 0.9 dynamic-slice_bitcast_fusion.5
  240.0 1.7 convolution_add_fusion.3
  241.7 0.9 dynamic-slice_bitcast_fusion.5
  243.0 1.7 convolution_add_fusion.3
  244.7 0.9 dynamic-slice_bitcast_fusion.5
  246.0 1.7 convolution_add_fusion.3
  247.7 0.9 dynamic-slice_bitcast_fusion.5
  249.1 1.7 convolution_add_fusion.3
  250.7 0.9 dynamic-slice_bitcast_fusion.5
  252.1 1.7 convolution_add_fusion.3
  253.8 0.9 dynamic-slice_bitcast_fusion.5
  255.1 1.7 convolution_add_fusion.3
  256.8 0.9 dynamic-slice_bitcast_fusion.5
  258.1 1.7 convolution_add_fusion.3
  259.8 0.9 dynamic-slice_bitcast_fusion.5
  261.1 1.7 convolution_add_fusion.3
  262.8 0.9 dynamic-slice_bitcast_fusion.5
  264.1 1.7 convolution_add_fusion.3
  265.8 0.9 dynamic-slice_bitcast_fusion.5
  267.1 1.7 convolution_add_fusion.3
  268.8 0.9 dynamic-slice_bitcast_fusion.5
  270.2 1.7 convolution_add_fusion.3
  271.8 0.9 dynamic-slice_bitcast_fusion.5
  273.2 1.7 convolution_add_fusion.3
  274.9 0.9 dynamic-slice_bitcast_fusion.5
  276.2 1.7 convolution_add_fusion.3
  277.9 0.9 dynamic-slice_bitcast_fusion.5
  279.2 1.7 convolution_add_fusion.3
  280.9 0.9 dynamic-slice_bitcast_fusion.5
  282.2 1.7 convolution_add_fusion.3
  285.2 1.7 convolution_add_fusion.3
  288.2 1.7 convolution_add_fusion.3
  291.3 1.7 convolution_add_fusion.3
  292.9 0.9 dynamic-slice_bitcast_fusion.5
  294.3 1.7 convolution_add_fusion.3
  297.3 1.7 convolution_add_fusion.3
  299.0 0.9 dynamic-slice_bitcast_fusion.5
  300.3 1.7 convolution_add_fusion.3
  302.0 0.9 dynamic-slice_bitcast_fusion.5
  303.3 1.7 convolution_add_fusion.3
  306.3 1.7 convolution_add_fusion.3
  308.0 0.9 dynamic-slice_bitcast_fusion.5
  309.3 1.7 convolution_add_fusion.3
  312.4 1.7 convolution_add_fusion.3
  314.1 0.9 dynamic-slice_bitcast_fusion.5
  315.4 1.7 convolution_add_fusion.3
  318.4 1.7 convolution_add_fusion.3
  320.1 13.5 %gather_fusion = bf16[384,512]{1,0:T(8,128)(2,1)S(1)} fusion(bf16[24576,512]{1,0:T(8,128)(2,1)} %get-tuple-element.239, s32[1024]{0:T(1024)S(1)} %pad_clamp_fusion), kind=kCustom, calls=%fused_computation | custom fusion | bytes 787968 | tf_op jit(solution)/shard_map/jit(_take)/gather | solution.py:59
  334.0 1.2 fusion.8
  (189 shorter events, 21.0 us)
Async XLA Ops:
  6.5 327.0 %copy-start = (bf16[512,512]{1,0:T(8,128)(2,1)S(1)}, bf16[512,512]{1,0:T(8,128)(2,1)}, u32[]{:S(2)}) copy-start(bf16[512,512]{1,0:T(8,128)(2,1)} %param.15) | copy-start | bytes 1572868
  6.5 35.3 %copy-start.2 = (s32[384]{0:T(512)S(1)}, s32[384]{0:T(512)}, u32[]{:S(2)}) copy-start(s32[384]{0:T(512)} %param.14) | copy-start | bytes 4612
  6.5 217.0 %all-gather.2.cloned.1.call-start = ((), (), s32[]{:S(2)}) async-start(), calls=%async_computation | async-start | bytes 25952256 | tf_op jit(solution)/shard_map/all_gather | solution.py:52
  36.1 5.8 %copy-start.1 = (bf16[3,32,2,128,128]{4,3,2,1,0:T(8,128)(2,1)S(1)}, bf16[3,32,2,128,128]{4,3,2,1,0:T(8,128)(2,1)}, u32[]{:S(2)}) copy-start(bf16[3,32,2,128,128]{4,3,2,1,0:T(8,128)(2,1)} %param.11) | copy-start | bytes 18874372
  223.6 110.4 %copy-start.3 = (bf16[512,512]{1,0:T(8,128)(2,1)S(1)}, bf16[512,512]{1,0:T(8,128)(2,1)}, u32[]{:S(2)}) copy-start(bf16[512,512]{1,0:T(8,128)(2,1)} %param.16) | copy-start | bytes 1572868
  223.6 110.4 %copy-start.4 = (f32[512]{0:T(512)S(1)}, f32[512]{0:T(512)}, u32[]{:S(2)}) copy-start(f32[512]{0:T(512)} %param.17) | copy-start | bytes 6148
Sparse Core Ops, SparseCore 0:
  34.3 189.1 all-gather.1
where the time goes:
time: 344 us; the launch traced here: 342 us
  waiting for transfers between devices  179 us (52%)
  matrix products  54.9 us (16%)
  local copies, waits for them, and re-layouts  45.8 us (13%)
  blocking collectives  27.6 us (8%)
  other arithmetic  19.7 us (6%)
  between operations  13.5 us (4%)
    all_gather x1, waiting for transfers between devices, on_device(): everything = lax.all_gather(panels, 'grp', axis=0, tiled=True)  179 us
    dot_general x32, matrix products, group_product(): return totals + jnp.dot(dense, window, preferred_element_type=jnp.float32)  53.3 us
    squeeze x32, local copies, waits for them, and re-layouts, dense_group(): values = lax.dynamic_index_in_dim(masked_values, group, 1, keepdims=False)  30.3 us
    all_gather x1, blocking collectives, on_device(): panels = lax.all_gather(features, 'rep', axis=0, tiled=True)  27.6 us
    gather x1, local copies, waits for them, and re-layouts, on_device(): own_rows = jnp.take(everything, state_ids, axis=0)  13.5 us
    add x32, other arithmetic, dense_group(): dense = dense + placed  7.71 us
  transfers between devices with their start and end apart: 1, of which 1 were waited for; matrix products, arithmetic and copies ran while one was open for 3% of the time, Pallas kernels for 0%

commit v1 on v0

--- a/solution.py
+++ b/solution.py
@@ -1,7 +1,17 @@
+import functools
 import jax
 import jax.numpy as jnp
 from jax import lax
 from jax.sharding import PartitionSpec as P
+
+
+def divide_the_field(obj, axis_k):
+    return jnp.concatenate(
+        lax.all_to_all(jnp.stack(lax.psum(1, "rep") * [obj], 0), "rep", 0, 0), axis_k
+    )
+
+
+direct_chains = functools.partial(divide_the_field, axis_k=0)
 
 
 def on_device(
@@ -14,7 +24,7 @@
     neighbour_weight,
     bias_vector,
 ):
-    panels = lax.all_gather(features, "rep", axis=0, tiled=True)
+    panels = direct_chains(features)
     row_blocks = tile_values.shape[0]
     group_count = tile_values.shape[1]
     slot_count = tile_values.shape[2]

time: 344 us -> 329 us (0.956)
  blocking collectives: 27.6 us -> 17.3 us
  waiting for transfers between devices: 179 us -> 173 us
    all_gather x1 -> x0, blocking collectives: 27.6 us -> none  [on_device(): panels = lax.all_gather(features, 'rep', axis=0, tiled=True)]
    all_to_all x0 -> x1, blocking collectives: none -> 17.3 us  [divide_the_field(): lax.all_to_all(jnp.stack(lax.psum(1, 'rep') * [obj], 0), 'rep', 0, 0)]
    all_gather x1, waiting for transfers between devices: 179 us -> 173 us  [on_device(): everything = lax.all_gather(panels, 'grp', axis=0, tiled=True)]
where the time goes in v1:
time: 329 us; the launch traced here: 327 us
  waiting for transfers between devices  173 us (53%)
  matrix products  54.9 us (17%)
  local copies, waits for them, and re-layouts  46.9 us (14%)
  other arithmetic  19.7 us (6%)
  blocking collectives  17.3 us (5%)
  between operations  13.5 us (4%)
    all_gather x1, waiting for transfers between devices, on_device(): everything = lax.all_gather(panels, 'grp', axis=0, tiled=True)  173 us
    dot_general x32, matrix products, group_product(): return totals + jnp.dot(dense, window, preferred_element_type=jnp.float32)  53.4 us
    squeeze x32, local copies, waits for them, and re-layouts, dense_group(): values = lax.dynamic_index_in_dim(masked_values, group, 1, keepdims=False)  30.3 us
    all_to_all x1, blocking collectives, divide_the_field(): lax.all_to_all(jnp.stack(lax.psum(1, 'rep') * [obj], 0), 'rep', 0, 0)  17.3 us
    gather x1, local copies, waits for them, and re-layouts, on_device(): own_rows = jnp.take(everything, state_ids, axis=0)  13.5 us
    add x32, other arithmetic, dense_group(): dense = dense + placed  7.71 us
  transfers between devices with their start and end apart: 1, of which 1 were waited for; matrix products, arithmetic and copies ran while one was open for 3% of the time, Pallas kernels for 0%

profile of v1, /device:TPU:1, one launch (start us, length us, event | category | flops | bytes accessed | tf_op | source)
XLA Modules:
  0.0 326.8 jit_solution(13558684867429153303)
XLA Ops:
  6.5 1.0 stack.2
  7.6 17.3 %all_to_all.5 = bf16[8,96,512]{2,1,0:T(8,128)(2,1)} all-to-all(bf16[8,96,512]{2,1,0:T(8,128)(2,1)S(1)} %stack.2), channel_id=1, replica_groups=mesh['grp'=32,'rep'=8] {'rep'}, dimensions={0} | all-to-all | bytes 1572864 | tf_op jit(solution)/shard_map/all_to_all | solution.py:10
  27.6 4.7 %convert_reduce_fusion = f32[3,32,2,128]{3,2,1,0:T(2,128)S(1)} fusion(bf16[3,32,2,128,128]{4,3,2,1,0:T(8,128)(2,1)} %param.11), kind=kLoop, calls=%fused_computation.15 | loop fusion | flops 6266880 | bytes 6389760 | tf_op jit(solution)/shard_map/reduce_sum | solution.py:38
  32.6 3.1 copy_select_fusion
  35.7 172.6 %all-gather.2.cloned.1.call-done = bf16[24576,512]{1,0:T(8,128)(2,1)} async-done(((bf16[768,512]{1,0:T(8,128)(2,1)}), bf16[24576,512]{1,0:T(8,128)(2,1)}) %all-gather.2.cloned.1.call-update) | async-done | bytes 25165840 | tf_op jit(solution)/shard_map/all_gather | solution.py:62
  208.3 96.5 %while.14 = (s32[]{:T(128)}, f32[384,512]{1,0:T(8,128)S(1)}, s32[3,32,2]{0,2,1:T(2,128)S(1)}, bf16[3,32,2,128,128]{4,3,0,2,1:T(8,128)(2,1)}, bf16[24576,512]{1,0...) while((s32[]{:T(128)}, f32[384,512]{1,0:T(8,128)S(1)}, ...), condition=%wide.region_1.2_spmd.clone, body=%wide.region_0.0_spmd.clone.sunk | while | flops 303267872 | bytes 4522361 | solution.py:68
  208.3 1.0 dynamic-slice_bitcast_fusion.5
  209.7 1.7 convolution_add_fusion.3
  211.4 0.9 dynamic-slice_bitcast_fusion.5
  212.7 1.7 convolution_add_fusion.3
  214.4 0.9 dynamic-slice_bitcast_fusion.5
  215.7 1.7 convolution_add_fusion.3
  217.4 0.9 dynamic-slice_bitcast_fusion.5
  218.7 1.7 convolution_add_fusion.3
  220.4 0.9 dynamic-slice_bitcast_fusion.5
  221.8 1.7 convolution_add_fusion.3
  223.4 0.9 dynamic-slice_bitcast_fusion.5
  224.8 1.7 convolution_add_fusion.3
  226.5 0.9 dynamic-slice_bitcast_fusion.5
  227.8 1.7 convolution_add_fusion.3
  229.5 0.9 dynamic-slice_bitcast_fusion.5
  230.8 1.7 convolution_add_fusion.3
  232.5 0.9 dynamic-slice_bitcast_fusion.5
  233.8 1.7 convolution_add_fusion.3
  235.5 0.9 dynamic-slice_bitcast_fusion.5
  236.8 1.7 convolution_add_fusion.3
  238.5 0.9 dynamic-slice_bitcast_fusion.5
  239.8 1.7 convolution_add_fusion.3
  241.5 0.9 dynamic-slice_bitcast_fusion.5
  242.9 1.7 convolution_add_fusion.3
  244.6 0.9 dynamic-slice_bitcast_fusion.5
  245.9 1.7 convolution_add_fusion.3
  247.6 0.9 dynamic-slice_bitcast_fusion.5
  248.9 1.7 convolution_add_fusion.3
  250.6 0.9 dynamic-slice_bitcast_fusion.5
  251.9 1.7 convolution_add_fusion.3
  253.6 0.9 dynamic-slice_bitcast_fusion.5
  254.9 1.7 convolution_add_fusion.3
  256.6 0.9 dynamic-slice_bitcast_fusion.5
  257.9 1.7 convolution_add_fusion.3
  259.6 0.9 dynamic-slice_bitcast_fusion.5
  260.9 1.7 convolution_add_fusion.3
  262.6 0.9 dynamic-slice_bitcast_fusion.5
  264.0 1.7 convolution_add_fusion.3
  265.7 0.9 dynamic-slice_bitcast_fusion.5
  267.0 1.7 convolution_add_fusion.3
  268.7 0.9 dynamic-slice_bitcast_fusion.5
  270.0 1.7 convolution_add_fusion.3
  273.0 1.7 convolution_add_fusion.3
  274.7 0.9 dynamic-slice_bitcast_fusion.5
  276.0 1.7 convolution_add_fusion.3
  279.0 1.7 convolution_add_fusion.3
  280.7 0.9 dynamic-slice_bitcast_fusion.5
  282.1 1.7 convolution_add_fusion.3
  285.1 1.7 convolution_add_fusion.3
  288.1 1.7 convolution_add_fusion.3
  291.1 1.7 convolution_add_fusion.3
  292.8 0.9 dynamic-slice_bitcast_fusion.5
  294.1 1.7 convolution_add_fusion.3
  297.1 1.7 convolution_add_fusion.3
  300.1 1.7 convolution_add_fusion.3
  303.2 1.7 convolution_add_fusion.3
  304.8 13.5 %gather_fusion = bf16[384,512]{1,0:T(8,128)(2,1)S(1)} fusion(bf16[24576,512]{1,0:T(8,128)(2,1)} %get-tuple-element.239, s32[1024]{0:T(1024)S(1)} %pad_clamp_fusion), kind=kCustom, calls=%fused_computation | custom fusion | bytes 787968 | tf_op jit(solution)/shard_map/jit(_take)/gather | solution.py:69
  318.8 1.2 fusion.8
  (190 shorter events, 22.0 us)
Async XLA Ops:
  6.5 311.8 %copy-start = (bf16[512,512]{1,0:T(8,128)(2,1)S(1)}, bf16[512,512]{1,0:T(8,128)(2,1)}, u32[]{:S(2)}) copy-start(bf16[512,512]{1,0:T(8,128)(2,1)} %param.15) | copy-start | bytes 1572868
  6.5 26.0 %copy-start.2 = (s32[384]{0:T(512)S(1)}, s32[384]{0:T(512)}, u32[]{:S(2)}) copy-start(s32[384]{0:T(512)} %param.14) | copy-start | bytes 4612
  6.5 201.8 %all-gather.2.cloned.1.call-start = ((), (), s32[]{:S(2)}) async-start(), calls=%async_computation.1 | async-start | bytes 25952256 | tf_op jit(solution)/shard_map/all_gather | solution.py:62
  26.8 5.8 %copy-start.1 = (bf16[3,32,2,128,128]{4,3,2,1,0:T(8,128)(2,1)S(1)}, bf16[3,32,2,128,128]{4,3,2,1,0:T(8,128)(2,1)}, u32[]{:S(2)}) copy-start(bf16[3,32,2,128,128]{4,3,2,1,0:T(8,128)(2,1)} %param.11) | copy-start | bytes 18874372
  208.3 110.4 %copy-start.3 = (bf16[512,512]{1,0:T(8,128)(2,1)S(1)}, bf16[512,512]{1,0:T(8,128)(2,1)}, u32[]{:S(2)}) copy-start(bf16[512,512]{1,0:T(8,128)(2,1)} %param.16) | copy-start | bytes 1572868
  208.3 110.4 %copy-start.4 = (f32[512]{0:T(512)S(1)}, f32[512]{0:T(512)}, u32[]{:S(2)}) copy-start(f32[512]{0:T(512)} %param.17) | copy-start | bytes 6148
Sparse Core Ops, SparseCore 0:
  25.0 183.2 all-gather.1
